TPU v7x, 32 devices: a whole 2x2x4 slice. The times are simulated.
32 devices in a mesh: row: 8 (over y, x, core), col: 4 (over z).
Axes of the slice: x: 2, y: 2, z: 4, core: 2. Of those that a mesh axis runs over, the one named last changes fastest.
Arguments:
- sub_basis: bfloat16 [32, 768, 768], P(('row', 'col')), may hold values from -0.15625 to 0.15625
- coupling: bfloat16 [32, 2, 768, 768], P(('row', 'col')), may hold values from -0.15625 to 0.15625
- pair_live: int32 [32, 2], P(('row', 'col')), may hold values 0 or 1
- offsets: int32 [32], P(('row', 'col')), may hold values from 0 to 3328
- dual_in: float32 [4, 4096], P('col', 'row'), may hold values from -6 to 6
Outputs:
- dual_out: float32 [4, 4096], P('col', 'row')
Inputs may be any that keep to these rules, and one draw needn't show every extreme that they name: `offsets`: each subdomain's window of 768 multipliers lies inside its block column's vector.
All inputs are finite; a program needn't handle non-finite values. No bound on the sum of `pair_live` on one device may be relied on, other than what follows from the above.
Results may differ from a plain program's by a relative error of at most 0.0085.
Values may be sent and summed in bfloat16 or wider, within the bound.
A program may use at most 64 MiB of HBM per device.

v0:
```python
import jax
import jax.numpy as jnp
from jax import lax
from jax.sharding import PartitionSpec as P


def passed_along(array, axis, by):
    count = lax.axis_size(axis)
    return lax.ppermute(array, axis, [(i, (i + by) % count) for i in range(count)])


def left_apply(matrix, vector):
    return lax.dot_general(
        matrix,
        vector,
        (((1,), (0,)), ((), ())),
        precision=lax.Precision.HIGHEST,
        preferred_element_type=jnp.float32,
    )


def right_apply(vector, matrix):
    return jnp.dot(
        vector, matrix, precision=lax.Precision.HIGHEST, preferred_element_type=jnp.float32
    )


def apply_dual(window, basis, couplings, live):
    projected = left_apply(basis, window)
    inner = projected
    summed = jnp.zeros_like(window)
    for slot, coupling in enumerate(couplings):
        distance = slot + 1
        ahead = passed_along(window, "col", -distance)
        inner = inner + live[slot] * left_apply(coupling, ahead)
        back = live[slot] * right_apply(projected, coupling)
        summed = summed + passed_along(back, "col", distance)
    return summed + right_apply(inner, basis)


def on_device(sub_basis, coupling, pair_live, offsets, dual_in):
    width = sub_basis.shape[2]
    basis = sub_basis[0].astype(jnp.float32)
    couplings = [coupling[0, h].astype(jnp.float32) for h in range(coupling.shape[1])]
    live = pair_live[0].astype(jnp.float32)
    length = dual_in.shape[1] * lax.axis_size("row")
    start = offsets[0]
    piece = dual_in
    for _ in range(2):
        column = lax.all_gather(piece, "row", axis=1, tiled=True)[0]
        window = lax.dynamic_slice_in_dim(column, start, width)
        local = apply_dual(window, basis, couplings, live)
        placed = lax.dynamic_update_slice(jnp.zeros((length,), jnp.float32), local, (start,))
        piece = lax.psum_scatter(placed[None, :], "row", scatter_dimension=1, tiled=True)
    return piece


def solution(mesh):
    return jax.shard_map(
        on_device,
        mesh=mesh,
        in_specs=(
            P(("row", "col"), None, None),
            P(("row", "col"), None, None, None),
            P(("row", "col"), None),
            P(("row", "col")),
            P("col", "row"),
        ),
        out_specs=P("col", "row"),
        check_vma=False,
    )
```

profile of v0, /device:TPU:0, one launch (start us, length us, event | category | flops | bytes accessed | tf_op | source)
XLA Modules:
  0.0 154.4 jit_solution(13610832899957684372)
XLA Ops:
  6.5 0.0 copy-start
  6.5 0.0 reduce-scatter.7.cloned.1.call-start
  7.3 10.5 %all_gather.6 = f32[1,4096]{1,0:T(1,128)S(1)} all-gather(f32[1,512]{1,0:T(1,128)} %param.9), channel_id=1, replica_groups=mesh['row'=8,'col'=4] {'row'}, dimensions={1}, use_global_device_ids=true | all-gather | bytes 18432 | tf_op jit(solution)/shard_map/all_gather | solution.py:50
  17.8 0.0 copy-start.2
  17.8 0.1 dynamic-slice_reduce_fusion.1
  17.9 0.0 copy-start.1
  17.9 3.7 %collective-permute-start.2 = (f32[768]{0:T(1024)S(1)}, f32[768]{0:T(1024)S(1)}, u32[]{:S(2)}, u32[]{:S(2)}) collective-permute-start(f32[768]{0:T(1024)S(1)} %dynamic-slice_reduce_fusion.1), channel_id=1, source_target_pairs={{0,3},{1,0},{2,1},{3,2},{4,7},{5,4},{6,5},{7,6},{8,11},{9,8},{10,9... | collective-permute-start | bytes 9224 | tf_op jit(solution)/shard_map/ppermute | solution.py:9
  21.5 0.0 collective-permute-start.3
  21.5 0.0 copy-done
  21.5 1.1 fusion.73
  22.6 0.0 copy-done.2
  22.7 0.6 fusion.72
  23.2 1.9 %fusion.30 = f32[768]{0:T(1024)S(1)} fusion(bf16[1,2,768,768]{3,2,1,0:T(8,128)(2,1)} %param.6, f32[1,768]{1,0:T(1,128)S(1)} %get-tuple-element.8), kind=kOutput, calls=%fused_computation.26 | convolution fusion | flops 7077888 | bytes 1185792 | tf_op jit(solution)/shard_map/dot_general | solution.py:23
  25.1 0.7 broadcast_multiply_fusion.3
  25.8 1.1 collective-permute-start
  26.8 0.0 copy-done.1
  26.8 0.6 fusion.42
  27.4 0.6 broadcast_multiply_fusion.1
  28.0 2.0 %collective-permute-start.1 = (f32[768]{0:T(1024)S(1)}, f32[768]{0:T(1024)S(1)}, u32[]{:S(2)}, u32[]{:S(2)}) collective-permute-start(f32[768]{0:T(1024)S(1)} %broadcast_multiply_fusion.1), channel_id=1, source_target_pairs={{0,2},{1,3},{2,0},{3,1},{4,6},{5,7},{6,4},{7,5},{8,10},{9,11},{10,... | collective-permute-start | bytes 9224 | tf_op jit(solution)/shard_map/ppermute | solution.py:9
  30.0 0.0 collective-permute-done.2
  30.0 1.1 fusion.33
  31.1 0.0 collective-permute-done.3
  31.1 1.1 fusion.45
  32.2 1.2 multiply_add_fusion.1
  33.4 0.6 fusion.24
  34.0 0.0 collective-permute-done
  34.0 0.0 collective-permute-done.1
  34.0 0.6 broadcast_in_dim.9
  34.6 0.8 dynamic_update_slice.8
  35.5 2.0 %copy.6 = f32[1,4096]{0,1:T(8,128)} copy(f32[1,4096]{1,0:T(1,128)S(1)} %dynamic_update_slice.8) | data formatting | bytes 32768
  37.5 0.0 reduce-scatter.7.cloned.1.call-update
  37.5 0.0 reduce-scatter.9.cloned.1.call-start
  37.5 41.0 %reduce-scatter.7.cloned.1.call-done = f32[512,1]{1,0:T(8,128)} async-done(((f32[4096,1]{1,0:T(8,128)}), f32[512,1]{1,0:T(8,128)}) %reduce-scatter.7.cloned.1.call-update) | async-done | bytes 2064
  78.6 1.1 copy.7
  79.6 8.8 %all_gather.7 = f32[1,4096]{1,0:T(1,128)S(1)} all-gather(f32[1,512]{1,0:T(1,128)S(1)} %copy.7), channel_id=1, replica_groups=mesh['row'=8,'col'=4] {'row'}, dimensions={1}, use_global_device_ids=true | all-gather | bytes 18432 | tf_op jit(solution)/shard_map/all_gather | solution.py:50
  88.5 0.1 dynamic-slice_reduce_fusion
  88.6 3.4 %collective-permute-start.6 = (f32[768]{0:T(1024)S(1)}, f32[768]{0:T(1024)S(1)}, u32[]{:S(2)}, u32[]{:S(2)}) collective-permute-start(f32[768]{0:T(1024)S(1)} %dynamic-slice_reduce_fusion), channel_id=1, source_target_pairs={{0,3},{1,0},{2,1},{3,2},{4,7},{5,4},{6,5},{7,6},{8,11},{9,8},{10,9... | collective-permute-start | bytes 9224 | tf_op jit(solution)/shard_map/ppermute | solution.py:9
  91.9 0.0 collective-permute-start.7
  91.9 1.1 fusion.74
  93.0 0.6 fusion.36
  93.6 0.6 fusion.48
  94.2 0.7 broadcast_multiply_fusion.2
  94.9 1.1 collective-permute-start.4
  96.0 0.6 broadcast_multiply_fusion
  96.6 1.9 %collective-permute-start.5 = (f32[768]{0:T(1024)S(1)}, f32[768]{0:T(1024)S(1)}, u32[]{:S(2)}, u32[]{:S(2)}) collective-permute-start(f32[768]{0:T(1024)S(1)} %broadcast_multiply_fusion), channel_id=1, source_target_pairs={{0,2},{1,3},{2,0},{3,1},{4,6},{5,7},{6,4},{7,5},{8,10},{9,11},{10,... | collective-permute-start | bytes 9224 | tf_op jit(solution)/shard_map/ppermute | solution.py:9
  98.5 0.0 collective-permute-done.6
  98.5 1.1 fusion.39
  99.6 0.0 collective-permute-done.7
  99.6 1.1 fusion.51
  100.7 1.2 multiply_add_fusion
  101.9 0.6 fusion.27
  102.5 0.0 collective-permute-done.4
  102.5 0.0 collective-permute-done.5
  102.6 0.2 dynamic_update_slice.9
  102.8 2.0 %copy.8 = f32[1,4096]{0,1:T(8,128)} copy(f32[1,4096]{1,0:T(1,128)S(1)} %dynamic_update_slice.9) | data formatting | bytes 32768
  104.8 0.0 reduce-scatter.9.cloned.1.call-update
  104.8 41.1 %reduce-scatter.9.cloned.1.call-done = f32[512,1]{1,0:T(8,128)} async-done(((f32[4096,1]{1,0:T(8,128)}), f32[512,1]{1,0:T(8,128)}) %reduce-scatter.9.cloned.1.call-update) | async-done | bytes 2064
  145.9 1.6 %copy.9 = f32[1,512]{1,0:T(1,128)} copy(f32[1,512]{0,1:T(8,128)} %bitcast.90) | data formatting | bytes 4096
  (12 shorter events, 0.1 us)
Async XLA Ops:
  6.5 15.0 %copy-start = (bf16[1,768,768]{2,1,0:T(8,128)(2,1)S(1)}, bf16[1,768,768]{2,1,0:T(8,128)(2,1)}, u32[]{:S(2)}) copy-start(bf16[1,768,768]{2,1,0:T(8,128)(2,1)} %param.5) | copy-start | bytes 3538948
  6.5 72.0 %reduce-scatter.7.cloned.1.call-start = ((), (), s32[]{:S(2)}) async-start(), calls=%async_computation.2 | async-start | bytes 2359296
  17.8 4.9 %copy-start.2 = (s32[1,2]{1,0:T(1,128)S(1)}, s32[1,2]{1,0:T(1,128)}, u32[]{:S(2)}) copy-start(s32[1,2]{1,0:T(1,128)} %param.7) | copy-start | bytes 28
  17.9 9.0 %copy-start.1 = (bf16[1,2,768,768]{3,2,1,0:T(8,128)(2,1)S(1)}, bf16[1,2,768,768]{3,2,1,0:T(8,128)(2,1)}, u32[]{:S(2)}) copy-start(bf16[1,2,768,768]{3,2,1,0:T(8,128)(2,1)} %param.6) | copy-start | bytes 7077892
  17.9 12.1 %collective-permute-start.2 = (f32[768]{0:T(1024)S(1)}, f32[768]{0:T(1024)S(1)}, u32[]{:S(2)}, u32[]{:S(2)}) collective-permute-start(f32[768]{0:T(1024)S(1)} %dynamic-slice_reduce_fusion.1), channel_id=1, source_target_pairs={{0,3},{1,0},{2,1},{3,2},{4,7},{5,4},{6,5},{7,6},{8,11},{9,8},{10,9... | collective-permute-start | bytes 9224 | tf_op jit(solution)/shard_map/ppermute | solution.py:9
  21.5 9.5 %collective-permute-start.3 = (f32[768]{0:T(1024)S(1)}, f32[768]{0:T(1024)S(1)}, u32[]{:S(2)}, u32[]{:S(2)}) collective-permute-start(f32[768]{0:T(1024)S(1)} %dynamic-slice_reduce_fusion.1), channel_id=1, source_target_pairs={{0,2},{1,3},{2,0},{3,1},{4,6},{5,7},{6,4},{7,5},{8,10},{9,11},{10,... | collective-permute-start | bytes 9224 | tf_op jit(solution)/shard_map/ppermute | solution.py:9
  25.8 8.2 %collective-permute-start = (f32[768]{0:T(1024)S(1)}, f32[768]{0:T(1024)S(1)}, u32[]{:S(2)}, u32[]{:S(2)}) collective-permute-start(f32[768]{0:T(1024)S(1)} %broadcast_multiply_fusion.3), channel_id=1, source_target_pairs={{0,1},{1,2},{2,3},{3,0},{4,5},{5,6},{6,7},{7,4},{8,9},{9,10},{10,1... | collective-permute-start | bytes 9224 | tf_op jit(solution)/shard_map/ppermute | solution.py:9
  28.0 6.0 %collective-permute-start.1 = (f32[768]{0:T(1024)S(1)}, f32[768]{0:T(1024)S(1)}, u32[]{:S(2)}, u32[]{:S(2)}) collective-permute-start(f32[768]{0:T(1024)S(1)} %broadcast_multiply_fusion.1), channel_id=1, source_target_pairs={{0,2},{1,3},{2,0},{3,1},{4,6},{5,7},{6,4},{7,5},{8,10},{9,11},{10,... | collective-permute-start | bytes 9224 | tf_op jit(solution)/shard_map/ppermute | solution.py:9
  37.5 108.4 %reduce-scatter.9.cloned.1.call-start = ((), (), s32[]{:S(2)}) async-start(), calls=%async_computation.3 | async-start | bytes 2359296
  88.6 10.0 %collective-permute-start.6 = (f32[768]{0:T(1024)S(1)}, f32[768]{0:T(1024)S(1)}, u32[]{:S(2)}, u32[]{:S(2)}) collective-permute-start(f32[768]{0:T(1024)S(1)} %dynamic-slice_reduce_fusion), channel_id=1, source_target_pairs={{0,3},{1,0},{2,1},{3,2},{4,7},{5,4},{6,5},{7,6},{8,11},{9,8},{10,9... | collective-permute-start | bytes 9224 | tf_op jit(solution)/shard_map/ppermute | solution.py:9
  91.9 7.7 %collective-permute-start.7 = (f32[768]{0:T(1024)S(1)}, f32[768]{0:T(1024)S(1)}, u32[]{:S(2)}, u32[]{:S(2)}) collective-permute-start(f32[768]{0:T(1024)S(1)} %dynamic-slice_reduce_fusion), channel_id=1, source_target_pairs={{0,2},{1,3},{2,0},{3,1},{4,6},{5,7},{6,4},{7,5},{8,10},{9,11},{10,... | collective-permute-start | bytes 9224 | tf_op jit(solution)/shard_map/ppermute | solution.py:9
  94.9 7.6 %collective-permute-start.4 = (f32[768]{0:T(1024)S(1)}, f32[768]{0:T(1024)S(1)}, u32[]{:S(2)}, u32[]{:S(2)}) collective-permute-start(f32[768]{0:T(1024)S(1)} %broadcast_multiply_fusion.2), channel_id=1, source_target_pairs={{0,1},{1,2},{2,3},{3,0},{4,5},{5,6},{6,7},{7,4},{8,9},{9,10},{10,1... | collective-permute-start | bytes 9224 | tf_op jit(solution)/shard_map/ppermute | solution.py:9
  96.6 5.9 %collective-permute-start.5 = (f32[768]{0:T(1024)S(1)}, f32[768]{0:T(1024)S(1)}, u32[]{:S(2)}, u32[]{:S(2)}) collective-permute-start(f32[768]{0:T(1024)S(1)} %broadcast_multiply_fusion), channel_id=1, source_target_pairs={{0,2},{1,3},{2,0},{3,1},{4,6},{5,7},{6,4},{7,5},{8,10},{9,11},{10,... | collective-permute-start | bytes 9224 | tf_op jit(solution)/shard_map/ppermute | solution.py:9
Sparse Core Ops, SparseCore 0:
  37.6 40.9 reduce-scatter.6
  104.9 40.9 reduce-scatter.8
where the time goes:
time: 155 us; the launch traced here: 154 us
  waiting for transfers between devices  82.2 us (53%)
  blocking collectives  19.3 us (12%)
  between operations  14.5 us (9%)
  starting transfers between devices  13.2 us (9%)
  matrix products  11.3 us (7%)
  local copies, waits for them, and re-layouts  9.11 us (6%)
  other arithmetic  4.85 us (3%)
    unnamed x4, waiting for transfers between devices  82.2 us
    all_gather x2, blocking collectives, on_device(): column = lax.all_gather(piece, 'row', axis=1, tiled=True)[0]  19.3 us
    ppermute x8, starting transfers between devices, passed_along(): lax.ppermute(array, axis, [(i, (i + by) % count) for i in range(count)])  13.1 us
    unnamed x10, local copies, waits for them, and re-layouts  6.72 us
    dot_general x6, matrix products, left_apply(): lax.dot_general(matrix, vector, (((1,), (0,)), ((), ())), precision=lax.P...  6.42 us
    dot_general x6, matrix products, right_apply(): jnp.dot(vector, matrix, precision=lax.Precision.HIGHEST, preferred_elemen...  4.84 us
  transfers between devices with their start and end apart: 10, of which 2 were waited for; matrix products, arithmetic and copies ran while one was open for 11% of the time, Pallas kernels for 0%

commit v1 on v0

--- a/solution.py
+++ b/solution.py
@@ -47,7 +47,25 @@
     start = offsets[0]
     piece = dual_in
     for _ in range(2):
-        column = lax.all_gather(piece, "row", axis=1, tiled=True)[0]
+
+        def _test_wall(original):
+            group_axis = "row"
+            q_n = lax.psum(1, axis_name=group_axis)
+            steps_seen = tuple(((b, (b + 1) % q_n) for b in range(q_n)))
+            trail = tuple(((b, (b - 1) % q_n) for b in range(q_n)))
+            heard, f_next = ([original], [original])
+            for _ in range(q_n // 2):
+                near = lax.ppermute(heard[-1], axis_name=group_axis, perm=steps_seen)
+                heard.append(near)
+            for _ in range((q_n - 1) // 2):
+                lower = lax.ppermute(f_next[-1], axis_name=group_axis, perm=trail)
+                f_next.append(lower)
+            base_arr = jnp.concatenate([*heard[::-1], *f_next[1:]], axis=1)
+            current_arr = lax.axis_index(group_axis)
+            front = jnp.roll(base_arr, shift=(current_arr - q_n // 2) * original.shape[1], axis=1)
+            return front
+
+        column = _test_wall(piece)[0]
         window = lax.dynamic_slice_in_dim(column, start, width)
         local = apply_dual(window, basis, couplings, live)
         placed = lax.dynamic_update_slice(jnp.zeros((length,), jnp.float32), local, (start,))

time: 155 us -> 168 us (1.084)
  blocking collectives: 19.3 us -> 0 us
  starting transfers between devices: 13.2 us -> 30.3 us
  waiting for transfers between devices: 82.2 us -> 96.3 us
    all_gather x2 -> x0, blocking collectives: 19.3 us -> none  [on_device(): column = lax.all_gather(piece, 'row', axis=1, tiled=True)[0]]
    ppermute x0 -> x14, starting transfers between devices: none -> 16.3 us  [the longest x6 15.8 us: _test_wall(): lower = lax.ppermute(f_next[-1], axis_name=group_axis, perm=trail)]
    ppermute x0 -> x14, waiting for transfers between devices: none -> 14 us  [the longest x8 13.9 us: _test_wall(): near = lax.ppermute(heard[-1], axis_name=group_axis, perm=steps_seen)]
    unnamed x10 -> x22, local copies, waits for them, and re-layouts: 6.72 us -> 7.49 us
  transfers between devices with their start and end apart: 10 -> 24, of which waited for: 2 -> 10; matrix products, arithmetic and copies ran while one was open for 11% -> 10% of each run, Pallas kernels for 0% -> 0%
where the time goes in v1:
time: 168 us
  waiting for transfers between devices  96.3 us (57%)
  starting transfers between devices  30.3 us (18%)
  between operations  14.4 us (9%)
  matrix products  11.3 us (7%)
  local copies, waits for them, and re-layouts  9.74 us (6%)
  other arithmetic  5.62 us (3%)
    unnamed x4, waiting for transfers between devices  82.3 us
    ppermute x6, starting transfers between devices, _test_wall(): lower = lax.ppermute(f_next[-1], axis_name=group_axis, perm=trail)  15.8 us
    ppermute x8, starting transfers between devices, passed_along(): lax.ppermute(array, axis, [(i, (i + by) % count) for i in range(count)])  13.9 us
    ppermute x8, waiting for transfers between devices, _test_wall(): near = lax.ppermute(heard[-1], axis_name=group_axis, perm=steps_seen)  13.9 us
    unnamed x22, local copies, waits for them, and re-layouts  7.49 us
    dot_general x6, matrix products, left_apply(): lax.dot_general(matrix, vector, (((1,), (0,)), ((), ())), precision=lax.P...  6.45 us
    dot_general x6, matrix products, right_apply(): jnp.dot(vector, matrix, precision=lax.Precision.HIGHEST, preferred_elemen...  4.84 us
  transfers between devices with their start and end apart: 24, of which 10 were waited for; matrix products, arithmetic and copies ran while one was open for 10% of the time, Pallas kernels for 0%

profile of v1, /device:TPU:0, one launch (start us, length us, event | category | flops | bytes accessed | tf_op | source)
XLA Modules:
  0.0 167.7 jit_solution(6566768334228420817)
XLA Ops:
  6.5 0.5 collective-permute-start
  7.0 4.4 %collective-permute-done = f32[1,512]{1,0:T(1,128)S(1)} collective-permute-done((f32[1,512]{1,0:T(1,128)}, f32[1,512]{1,0:T(1,128)S(1)}, u32[]{:S(2)}, u32[]{:S(2)}) %collective-permute-start) | collective-permute-done | bytes 2080 | tf_op jit(solution)/shard_map/ppermute | solution.py:58
  11.4 0.0 collective-permute-start.1
  11.4 2.6 %collective-permute-start.4 = (f32[1,512]{1,0:T(1,128)}, f32[1,512]{1,0:T(1,128)S(1)}, u32[]{:S(2)}, u32[]{:S(2)}) collective-permute-start(f32[1,512]{1,0:T(1,128)} %param.11), channel_id=1, source_target_pairs={{0,28},{4,0},{8,4},{12,8},{16,12},{20,16},{24,20},{28,24},{1,29},{... | collective-permute-start | bytes 6152 | tf_op jit(solution)/shard_map/ppermute | solution.py:61
  14.0 0.7 convert_element_type.3
  14.7 0.6 collective-permute-done.1
  15.3 0.0 collective-permute-start.2
  15.3 0.6 fusion.74
  15.9 0.0 collective-permute-done.4
  15.9 2.6 %collective-permute-start.5 = (f32[1,512]{1,0:T(1,128)S(1)}, f32[1,512]{1,0:T(1,128)S(1)}, u32[]{:S(2)}, u32[]{:S(2)}) collective-permute-start(f32[1,512]{1,0:T(1,128)S(1)} %collective-permute-done.4), channel_id=1, source_target_pairs={{0,28},{4,0},{8,4},{12,8},{16,12},{20,16},{24,20},{28,24},{1,29},{... | collective-permute-start | bytes 6152 | tf_op jit(solution)/shard_map/ppermute | solution.py:61
  18.5 0.7 collective-permute-done.2
  19.8 2.7 %collective-permute-start.6 = (f32[1,512]{1,0:T(1,128)S(1)}, f32[1,512]{1,0:T(1,128)S(1)}, u32[]{:S(2)}, u32[]{:S(2)}) collective-permute-start(f32[1,512]{1,0:T(1,128)S(1)} %collective-permute-done.5), channel_id=1, source_target_pairs={{0,28},{4,0},{8,4},{12,8},{16,12},{20,16},{24,20},{28,24},{1,29},{... | collective-permute-start | bytes 6152 | tf_op jit(solution)/shard_map/ppermute | solution.py:61
  22.5 0.5 collective-permute-done.3
  23.1 0.7 constant_dynamic-update-slice_fusion.3
  23.8 0.0 collective-permute-done.6
  23.9 0.1 fusion.70
  24.0 0.0 copy-start.1
  24.0 4.4 %collective-permute-start.9 = (f32[768]{0:T(1024)S(1)}, f32[768]{0:T(1024)S(1)}, u32[]{:S(2)}, u32[]{:S(2)}) collective-permute-start(f32[768]{0:T(1024)S(1)} %fusion.70), channel_id=1, source_target_pairs={{0,3},{1,0},{2,1},{3,2},{4,7},{5,4},{6,5},{7,6},{8,11},{9,8},{10,9... | collective-permute-start | bytes 9224 | tf_op jit(solution)/shard_map/ppermute | solution.py:9
  28.4 1.1 fusion.75
  29.5 1.9 %fusion.30 = f32[768]{0:T(1024)S(1)} fusion(bf16[1,2,768,768]{3,2,1,0:T(8,128)(2,1)} %param.8, f32[1,768]{1,0:T(1,128)S(1)} %get-tuple-element.9), kind=kOutput, calls=%fused_computation.26 | convolution fusion | flops 7077888 | bytes 1185792 | tf_op jit(solution)/shard_map/dot_general | solution.py:23
  31.4 0.6 fusion.42
  32.0 0.6 broadcast_multiply_fusion.3
  32.5 1.1 collective-permute-start.7
  33.6 0.6 broadcast_multiply_fusion.1
  34.2 2.0 %collective-permute-start.8 = (f32[768]{0:T(1024)S(1)}, f32[768]{0:T(1024)S(1)}, u32[]{:S(2)}, u32[]{:S(2)}) collective-permute-start(f32[768]{0:T(1024)S(1)} %broadcast_multiply_fusion.1), channel_id=1, source_target_pairs={{0,2},{1,3},{2,0},{3,1},{4,6},{5,7},{6,4},{7,5},{8,10},{9,11},{10,... | collective-permute-start | bytes 9224 | tf_op jit(solution)/shard_map/ppermute | solution.py:9
  36.2 1.1 fusion.33
  37.3 1.1 fusion.45
  38.4 1.2 multiply_add_fusion.1
  39.6 0.6 fusion.24
  40.3 0.6 broadcast_in_dim.9
  40.9 0.8 dynamic_update_slice.8
  41.7 2.0 %copy.6 = f32[1,4096]{0,1:T(8,128)} copy(f32[1,4096]{1,0:T(1,128)S(1)} %dynamic_update_slice.8) | data formatting | bytes 32768
  43.7 0.0 reduce-scatter.7.cloned.1.call-update
  43.7 0.0 reduce-scatter.9.cloned.1.call-start
  43.8 41.1 %reduce-scatter.7.cloned.1.call-done = f32[512,1]{1,0:T(8,128)} async-done(((f32[4096,1]{1,0:T(8,128)}), f32[512,1]{1,0:T(8,128)}) %reduce-scatter.7.cloned.1.call-update) | async-done | bytes 2064
  84.9 1.1 copy.7
  86.0 0.0 collective-permute-start.11
  86.0 3.9 %collective-permute-done.11 = f32[1,512]{1,0:T(1,128)S(1)} collective-permute-done((f32[1,512]{1,0:T(1,128)S(1)}, f32[1,512]{1,0:T(1,128)S(1)}, u32[]{:S(2)}, u32[]{:S(2)}) %collective-permute-start.11) | collective-permute-done | bytes 2080 | tf_op jit(solution)/shard_map/ppermute | solution.py:58
  89.9 2.6 %collective-permute-start.15 = (f32[1,512]{1,0:T(1,128)S(1)}, f32[1,512]{1,0:T(1,128)S(1)}, u32[]{:S(2)}, u32[]{:S(2)}) collective-permute-start(f32[1,512]{1,0:T(1,128)S(1)} %copy.7), channel_id=1, source_target_pairs={{0,28},{4,0},{8,4},{12,8},{16,12},{20,16},{24,20},{28,24},{1,29},{... | collective-permute-start | bytes 6152 | tf_op jit(solution)/shard_map/ppermute | solution.py:61
  92.5 1.3 collective-permute-done.12
  93.8 0.0 collective-permute-done.15
  93.9 2.6 %collective-permute-start.16 = (f32[1,512]{1,0:T(1,128)S(1)}, f32[1,512]{1,0:T(1,128)S(1)}, u32[]{:S(2)}, u32[]{:S(2)}) collective-permute-start(f32[1,512]{1,0:T(1,128)S(1)} %collective-permute-done.15), channel_id=1, source_target_pairs={{0,28},{4,0},{8,4},{12,8},{16,12},{20,16},{24,20},{28,24},{1,29},{... | collective-permute-start | bytes 6152 | tf_op jit(solution)/shard_map/ppermute | solution.py:61
  96.5 1.3 collective-permute-done.13
  97.7 0.0 collective-permute-done.16
  97.8 2.6 %collective-permute-start.17 = (f32[1,512]{1,0:T(1,128)S(1)}, f32[1,512]{1,0:T(1,128)S(1)}, u32[]{:S(2)}, u32[]{:S(2)}) collective-permute-start(f32[1,512]{1,0:T(1,128)S(1)} %collective-permute-done.16), channel_id=1, source_target_pairs={{0,28},{4,0},{8,4},{12,8},{16,12},{20,16},{24,20},{28,24},{1,29},{... | collective-permute-start | bytes 6152 | tf_op jit(solution)/shard_map/ppermute | solution.py:61
  100.4 1.3 collective-permute-done.14
  101.7 1.1 fusion.76
  102.8 0.1 fusion.72
  102.9 3.4 %collective-permute-start.20 = (f32[768]{0:T(1024)S(1)}, f32[768]{0:T(1024)S(1)}, u32[]{:S(2)}, u32[]{:S(2)}) collective-permute-start(f32[768]{0:T(1024)S(1)} %fusion.72), channel_id=1, source_target_pairs={{0,3},{1,0},{2,1},{3,2},{4,7},{5,4},{6,5},{7,6},{8,11},{9,8},{10,9... | collective-permute-start | bytes 9224 | tf_op jit(solution)/shard_map/ppermute | solution.py:9
  106.3 0.6 fusion.36
  106.9 0.6 fusion.48
  107.5 0.6 broadcast_multiply_fusion.2
  108.1 1.2 collective-permute-start.18
  109.3 0.6 broadcast_multiply_fusion
  109.9 1.9 %collective-permute-start.19 = (f32[768]{0:T(1024)S(1)}, f32[768]{0:T(1024)S(1)}, u32[]{:S(2)}, u32[]{:S(2)}) collective-permute-start(f32[768]{0:T(1024)S(1)} %broadcast_multiply_fusion), channel_id=1, source_target_pairs={{0,2},{1,3},{2,0},{3,1},{4,6},{5,7},{6,4},{7,5},{8,10},{9,11},{10,... | collective-permute-start | bytes 9224 | tf_op jit(solution)/shard_map/ppermute | solution.py:9
  111.8 1.1 fusion.39
  112.9 1.1 fusion.51
  114.0 1.2 multiply_add_fusion
  115.2 0.6 fusion.27
  115.8 0.2 dynamic_update_slice.9
  116.0 2.0 %copy.8 = f32[1,4096]{0,1:T(8,128)} copy(f32[1,4096]{1,0:T(1,128)S(1)} %dynamic_update_slice.9) | data formatting | bytes 32768
  118.0 0.0 reduce-scatter.9.cloned.1.call-update
  118.0 41.2 %reduce-scatter.9.cloned.1.call-done = f32[512,1]{1,0:T(8,128)} async-done(((f32[4096,1]{1,0:T(8,128)}), f32[512,1]{1,0:T(8,128)}) %reduce-scatter.9.cloned.1.call-update) | async-done | bytes 2064
  159.2 1.6 copy.9
  (46 shorter events, 0.2 us)
Async XLA Ops:
  6.5 21.9 %copy-start = (bf16[1,768,768]{2,1,0:T(8,128)(2,1)S(1)}, bf16[1,768,768]{2,1,0:T(8,128)(2,1)}, u32[]{:S(2)}) copy-start(bf16[1,768,768]{2,1,0:T(8,128)(2,1)} %param.7) | copy-start | bytes 3538948
  6.5 78.4 %reduce-scatter.7.cloned.1.call-start = ((), (), s32[]{:S(2)}) async-start(), calls=%async_computation.2 | async-start | bytes 2359296
  6.5 4.8 %collective-permute-start = (f32[1,512]{1,0:T(1,128)}, f32[1,512]{1,0:T(1,128)S(1)}, u32[]{:S(2)}, u32[]{:S(2)}) collective-permute-start(f32[1,512]{1,0:T(1,128)} %param.11), channel_id=1, source_target_pairs={{0,4},{4,8},{8,12},{12,16},{16,20},{20,24},{24,28},{28,0},{1,5},{5... | collective-permute-start | bytes 6152 | tf_op jit(solution)/shard_map/ppermute | solution.py:58
  11.4 3.9 %collective-permute-start.1 = (f32[1,512]{1,0:T(1,128)S(1)}, f32[1,512]{1,0:T(1,128)S(1)}, u32[]{:S(2)}, u32[]{:S(2)}) collective-permute-start(f32[1,512]{1,0:T(1,128)S(1)} %collective-permute-done), channel_id=1, source_target_pairs={{0,4},{4,8},{8,12},{12,16},{16,20},{20,24},{24,28},{28,0},{1,5},{5... | collective-permute-start | bytes 6152 | tf_op jit(solution)/shard_map/ppermute | solution.py:58
  11.4 4.5 %collective-permute-start.4 = (f32[1,512]{1,0:T(1,128)}, f32[1,512]{1,0:T(1,128)S(1)}, u32[]{:S(2)}, u32[]{:S(2)}) collective-permute-start(f32[1,512]{1,0:T(1,128)} %param.11), channel_id=1, source_target_pairs={{0,28},{4,0},{8,4},{12,8},{16,12},{20,16},{24,20},{28,24},{1,29},{... | collective-permute-start | bytes 6152 | tf_op jit(solution)/shard_map/ppermute | solution.py:61
  15.3 3.9 %collective-permute-start.2 = (f32[1,512]{1,0:T(1,128)S(1)}, f32[1,512]{1,0:T(1,128)S(1)}, u32[]{:S(2)}, u32[]{:S(2)}) collective-permute-start(f32[1,512]{1,0:T(1,128)S(1)} %collective-permute-done.1), channel_id=1, source_target_pairs={{0,4},{4,8},{8,12},{12,16},{16,20},{20,24},{24,28},{28,0},{1,5},{5... | collective-permute-start | bytes 6152 | tf_op jit(solution)/shard_map/ppermute | solution.py:58
  15.9 4.0 %collective-permute-start.5 = (f32[1,512]{1,0:T(1,128)S(1)}, f32[1,512]{1,0:T(1,128)S(1)}, u32[]{:S(2)}, u32[]{:S(2)}) collective-permute-start(f32[1,512]{1,0:T(1,128)S(1)} %collective-permute-done.4), channel_id=1, source_target_pairs={{0,28},{4,0},{8,4},{12,8},{16,12},{20,16},{24,20},{28,24},{1,29},{... | collective-permute-start | bytes 6152 | tf_op jit(solution)/shard_map/ppermute | solution.py:61
  19.2 3.9 %collective-permute-start.3 = (f32[1,512]{1,0:T(1,128)S(1)}, f32[1,512]{1,0:T(1,128)S(1)}, u32[]{:S(2)}, u32[]{:S(2)}) collective-permute-start(f32[1,512]{1,0:T(1,128)S(1)} %collective-permute-done.2), channel_id=1, source_target_pairs={{0,4},{4,8},{8,12},{12,16},{16,20},{20,24},{24,28},{28,0},{1,5},{5... | collective-permute-start | bytes 6152 | tf_op jit(solution)/shard_map/ppermute | solution.py:58
  19.8 4.0 %collective-permute-start.6 = (f32[1,512]{1,0:T(1,128)S(1)}, f32[1,512]{1,0:T(1,128)S(1)}, u32[]{:S(2)}, u32[]{:S(2)}) collective-permute-start(f32[1,512]{1,0:T(1,128)S(1)} %collective-permute-done.5), channel_id=1, source_target_pairs={{0,28},{4,0},{8,4},{12,8},{16,12},{20,16},{24,20},{28,24},{1,29},{... | collective-permute-start | bytes 6152 | tf_op jit(solution)/shard_map/ppermute | solution.py:61
  24.0 7.4 %copy-start.1 = (bf16[1,2,768,768]{3,2,1,0:T(8,128)(2,1)S(1)}, bf16[1,2,768,768]{3,2,1,0:T(8,128)(2,1)}, u32[]{:S(2)}) copy-start(bf16[1,2,768,768]{3,2,1,0:T(8,128)(2,1)} %param.8) | copy-start | bytes 7077892
  24.0 12.3 %collective-permute-start.9 = (f32[768]{0:T(1024)S(1)}, f32[768]{0:T(1024)S(1)}, u32[]{:S(2)}, u32[]{:S(2)}) collective-permute-start(f32[768]{0:T(1024)S(1)} %fusion.70), channel_id=1, source_target_pairs={{0,3},{1,0},{2,1},{3,2},{4,7},{5,4},{6,5},{7,6},{8,11},{9,8},{10,9... | collective-permute-start | bytes 9224 | tf_op jit(solution)/shard_map/ppermute | solution.py:9
  28.4 8.9 %collective-permute-start.10 = (f32[768]{0:T(1024)S(1)}, f32[768]{0:T(1024)S(1)}, u32[]{:S(2)}, u32[]{:S(2)}) collective-permute-start(f32[768]{0:T(1024)S(1)} %fusion.70), channel_id=1, source_target_pairs={{0,2},{1,3},{2,0},{3,1},{4,6},{5,7},{6,4},{7,5},{8,10},{9,11},{10,... | collective-permute-start | bytes 9224 | tf_op jit(solution)/shard_map/ppermute | solution.py:9
  32.5 7.7 %collective-permute-start.7 = (f32[768]{0:T(1024)S(1)}, f32[768]{0:T(1024)S(1)}, u32[]{:S(2)}, u32[]{:S(2)}) collective-permute-start(f32[768]{0:T(1024)S(1)} %broadcast_multiply_fusion.3), channel_id=1, source_target_pairs={{0,1},{1,2},{2,3},{3,0},{4,5},{5,6},{6,7},{7,4},{8,9},{9,10},{10,1... | collective-permute-start | bytes 9224 | tf_op jit(solution)/shard_map/ppermute | solution.py:9
  34.2 6.0 %collective-permute-start.8 = (f32[768]{0:T(1024)S(1)}, f32[768]{0:T(1024)S(1)}, u32[]{:S(2)}, u32[]{:S(2)}) collective-permute-start(f32[768]{0:T(1024)S(1)} %broadcast_multiply_fusion.1), channel_id=1, source_target_pairs={{0,2},{1,3},{2,0},{3,1},{4,6},{5,7},{6,4},{7,5},{8,10},{9,11},{10,... | collective-permute-start | bytes 9224 | tf_op jit(solution)/shard_map/ppermute | solution.py:9
  43.7 115.5 %reduce-scatter.9.cloned.1.call-start = ((), (), s32[]{:S(2)}) async-start(), calls=%async_computation.3 | async-start | bytes 2359296
  86.0 3.9 %collective-permute-start.11 = (f32[1,512]{1,0:T(1,128)S(1)}, f32[1,512]{1,0:T(1,128)S(1)}, u32[]{:S(2)}, u32[]{:S(2)}) collective-permute-start(f32[1,512]{1,0:T(1,128)S(1)} %copy.7), channel_id=1, source_target_pairs={{0,4},{4,8},{8,12},{12,16},{16,20},{20,24},{24,28},{28,0},{1,5},{5... | collective-permute-start | bytes 6152 | tf_op jit(solution)/shard_map/ppermute | solution.py:58
  89.9 3.9 %collective-permute-start.12 = (f32[1,512]{1,0:T(1,128)S(1)}, f32[1,512]{1,0:T(1,128)S(1)}, u32[]{:S(2)}, u32[]{:S(2)}) collective-permute-start(f32[1,512]{1,0:T(1,128)S(1)} %collective-permute-done.11), channel_id=1, source_target_pairs={{0,4},{4,8},{8,12},{12,16},{16,20},{20,24},{24,28},{28,0},{1,5},{5... | collective-permute-start | bytes 6152 | tf_op jit(solution)/shard_map/ppermute | solution.py:58
  89.9 4.0 %collective-permute-start.15 = (f32[1,512]{1,0:T(1,128)S(1)}, f32[1,512]{1,0:T(1,128)S(1)}, u32[]{:S(2)}, u32[]{:S(2)}) collective-permute-start(f32[1,512]{1,0:T(1,128)S(1)} %copy.7), channel_id=1, source_target_pairs={{0,28},{4,0},{8,4},{12,8},{16,12},{20,16},{24,20},{28,24},{1,29},{... | collective-permute-start | bytes 6152 | tf_op jit(solution)/shard_map/ppermute | solution.py:61
  93.8 3.9 %collective-permute-start.13 = (f32[1,512]{1,0:T(1,128)S(1)}, f32[1,512]{1,0:T(1,128)S(1)}, u32[]{:S(2)}, u32[]{:S(2)}) collective-permute-start(f32[1,512]{1,0:T(1,128)S(1)} %collective-permute-done.12), channel_id=1, source_target_pairs={{0,4},{4,8},{8,12},{12,16},{16,20},{20,24},{24,28},{28,0},{1,5},{5... | collective-permute-start | bytes 6152 | tf_op jit(solution)/shard_map/ppermute | solution.py:58
  93.9 3.9 %collective-permute-start.16 = (f32[1,512]{1,0:T(1,128)S(1)}, f32[1,512]{1,0:T(1,128)S(1)}, u32[]{:S(2)}, u32[]{:S(2)}) collective-permute-start(f32[1,512]{1,0:T(1,128)S(1)} %collective-permute-done.15), channel_id=1, source_target_pairs={{0,28},{4,0},{8,4},{12,8},{16,12},{20,16},{24,20},{28,24},{1,29},{... | collective-permute-start | bytes 6152 | tf_op jit(solution)/shard_map/ppermute | solution.py:61
  97.7 3.9 %collective-permute-start.14 = (f32[1,512]{1,0:T(1,128)S(1)}, f32[1,512]{1,0:T(1,128)S(1)}, u32[]{:S(2)}, u32[]{:S(2)}) collective-permute-start(f32[1,512]{1,0:T(1,128)S(1)} %collective-permute-done.13), channel_id=1, source_target_pairs={{0,4},{4,8},{8,12},{12,16},{16,20},{20,24},{24,28},{28,0},{1,5},{5... | collective-permute-start | bytes 6152 | tf_op jit(solution)/shard_map/ppermute | solution.py:58
  97.8 3.9 %collective-permute-start.17 = (f32[1,512]{1,0:T(1,128)S(1)}, f32[1,512]{1,0:T(1,128)S(1)}, u32[]{:S(2)}, u32[]{:S(2)}) collective-permute-start(f32[1,512]{1,0:T(1,128)S(1)} %collective-permute-done.16), channel_id=1, source_target_pairs={{0,28},{4,0},{8,4},{12,8},{16,12},{20,16},{24,20},{28,24},{1,29},{... | collective-permute-start | bytes 6152 | tf_op jit(solution)/shard_map/ppermute | solution.py:61
  102.9 8.8 %collective-permute-start.20 = (f32[768]{0:T(1024)S(1)}, f32[768]{0:T(1024)S(1)}, u32[]{:S(2)}, u32[]{:S(2)}) collective-permute-start(f32[768]{0:T(1024)S(1)} %fusion.72), channel_id=1, source_target_pairs={{0,3},{1,0},{2,1},{3,2},{4,7},{5,4},{6,5},{7,6},{8,11},{9,8},{10,9... | collective-permute-start | bytes 9224 | tf_op jit(solution)/shard_map/ppermute | solution.py:9
  106.3 6.5 %collective-permute-start.21 = (f32[768]{0:T(1024)S(1)}, f32[768]{0:T(1024)S(1)}, u32[]{:S(2)}, u32[]{:S(2)}) collective-permute-start(f32[768]{0:T(1024)S(1)} %fusion.72), channel_id=1, source_target_pairs={{0,2},{1,3},{2,0},{3,1},{4,6},{5,7},{6,4},{7,5},{8,10},{9,11},{10,... | collective-permute-start | bytes 9224 | tf_op jit(solution)/shard_map/ppermute | solution.py:9
  108.1 7.7 %collective-permute-start.18 = (f32[768]{0:T(1024)S(1)}, f32[768]{0:T(1024)S(1)}, u32[]{:S(2)}, u32[]{:S(2)}) collective-permute-start(f32[768]{0:T(1024)S(1)} %broadcast_multiply_fusion.2), channel_id=1, source_target_pairs={{0,1},{1,2},{2,3},{3,0},{4,5},{5,6},{6,7},{7,4},{8,9},{9,10},{10,1... | collective-permute-start | bytes 9224 | tf_op jit(solution)/shard_map/ppermute | solution.py:9
  109.9 5.9 %collective-permute-start.19 = (f32[768]{0:T(1024)S(1)}, f32[768]{0:T(1024)S(1)}, u32[]{:S(2)}, u32[]{:S(2)}) collective-permute-start(f32[768]{0:T(1024)S(1)} %broadcast_multiply_fusion), channel_id=1, source_target_pairs={{0,2},{1,3},{2,0},{3,1},{4,6},{5,7},{6,4},{7,5},{8,10},{9,11},{10,... | collective-permute-start | bytes 9224 | tf_op jit(solution)/shard_map/ppermute | solution.py:9
Sparse Core Ops, SparseCore 0:
  43.8 41.0 reduce-scatter.6
  118.2 40.9 reduce-scatter.8
